TPU v7x, 32 devices: a whole 2x2x4 slice. The times are simulated.
32 devices in a mesh: fsdp: 8 (over y, x, core), tp: 4 (over z).
Axes of the slice: x: 2, y: 2, z: 4, core: 2. Of those that a mesh axis runs over, the one named last changes fastest.
Arguments:
- tokens: bfloat16 [8192, 2048], P(('fsdp', 'tp')), may hold values from -6 to 6
- norm1_gain: float32 [2048], replicated, may hold values from 0.25 to 1.75
- norm1_shift: float32 [2048], replicated, may hold values from -1 to 1
- w_query: bfloat16 [2048, 2048], P('fsdp', 'tp'), may hold values from -0.125 to 0.125
- b_query: float32 [2048], P('tp'), may hold values from -1 to 1
- w_key: bfloat16 [2048, 2048], P('fsdp', 'tp'), may hold values from -0.125 to 0.125
- w_value: bfloat16 [2048, 2048], P('fsdp', 'tp'), may hold values from -0.125 to 0.125
- b_value: float32 [2048], P('tp'), may hold values from -1 to 1
- w_out: bfloat16 [2048, 2048], P('fsdp', 'tp'), may hold values from -0.5 to 0.5
- b_out: float32 [2048], replicated, may hold values from -1 to 1
- norm2_gain: float32 [2048], replicated, may hold values from 0.25 to 1.75
- norm2_shift: float32 [2048], replicated, may hold values from -1 to 1
- w_up: bfloat16 [2048, 8192], P('fsdp', 'tp'), may hold values from -0.125 to 0.125
- b_up: float32 [8192], P('tp'), may hold values from -1 to 1
- w_down: bfloat16 [2048, 8192], P('fsdp', 'tp'), may hold values from -0.09375 to 0.09375
- b_down: float32 [2048], replicated, may hold values from -1 to 1
- teacher: bfloat16 [8192, 2048], P(('fsdp', 'tp')), may hold values from -6 to 6
- valid_mask: int32 [8192], P(('fsdp', 'tp')), may hold values from 0 to 1, as said below
- parents: int32 [8, 8], P('fsdp'), may hold values from -1 to 6, as said below
- summary: int32 [8, 8, 12], P('fsdp'), may hold values from 0 to 127, as said below
Outputs:
- output_states: bfloat16 [8192, 2048], P(('fsdp', 'tp'))
- mean_loss: float32 [], replicated
- grad_tokens: float32 [8192, 2048], P(('fsdp', 'tp'))
- grad_norm1_gain: float32 [2048], replicated
- grad_norm1_shift: float32 [2048], replicated
- grad_w_query: float32 [2048, 2048], P('fsdp', 'tp')
- grad_b_query: float32 [2048], P('tp')
- grad_w_key: float32 [2048, 2048], P('fsdp', 'tp')
- grad_w_value: float32 [2048, 2048], P('fsdp', 'tp')
- grad_b_value: float32 [2048], P('tp')
- grad_w_out: float32 [2048, 2048], P('fsdp', 'tp')
- grad_b_out: float32 [2048], replicated
- grad_norm2_gain: float32 [2048], replicated
- grad_norm2_shift: float32 [2048], replicated
- grad_w_up: float32 [2048, 8192], P('fsdp', 'tp')
- grad_b_up: float32 [8192], P('tp')
- grad_w_down: float32 [2048, 8192], P('fsdp', 'tp')
- grad_b_down: float32 [2048], replicated
Inputs may be any that keep to these rules, and one draw needn't show every extreme that they name: valid_mask is 1 at the first token of every tree. parents[f, 0] is -1 and 0 <= parents[f, s] < s for every later segment s; the last segment of every tree has the segment before it as parent. `summary`: the 12 offsets of one segment are distinct.
All inputs are finite; a program needn't handle non-finite values.
Results may differ from a plain program's by a relative error of at most 0.019.
Values may be sent and summed in bfloat16 or wider, within the bound.
No kernel may reach another device: no remote copies, remote signals or barrier semaphores. Data moves between devices by JAX's collectives and lax.ppermute only.
A program may use at most 192 MiB of HBM per device.

v0:
```python
import jax
import jax.numpy as jnp
from jax import lax
from jax.sharding import PartitionSpec as P

HD = 64
EPSILON = 1e-05
MASKED_SCORE = -1e30


def layer_norm(vectors, norm_gain, norm_shift):
    centre = jnp.mean(vectors, axis=-1, keepdims=True)
    centred = vectors - centre
    spread = jnp.mean(centred * centred, axis=-1, keepdims=True)
    return centred * lax.rsqrt(spread + EPSILON) * norm_gain + norm_shift


def ancestors(parent_row):
    segments = parent_row.shape[0]
    columns = jnp.arange(segments, dtype=jnp.int32)

    def follow(sweep, state_pair):
        ancestry, current = state_pair
        matches = current[:, None] == columns[None, :]
        ancestry = jnp.maximum(ancestry, matches.astype(jnp.float32))
        following = jnp.sum(jnp.where(matches, parent_row[None, :], 0), axis=1)
        current = jnp.where(current >= 0, following, -1)
        return (ancestry, current)

    start_table = jnp.zeros((segments, segments), jnp.float32)
    ancestry, finished = lax.fori_loop(0, segments, follow, (start_table, parent_row))
    return ancestry


def tree_tables(parent_row, summary_rows, length):
    segments = parent_row.shape[0]
    seg_length = length // segments
    ancestry = ancestors(parent_row)
    offsets = jnp.arange(seg_length, dtype=jnp.int32)
    marked = jnp.max(
        (summary_rows[:, :, None] == offsets[None, None, :]).astype(jnp.float32), axis=1
    ).reshape(length)
    key_segment = jnp.arange(length, dtype=jnp.int32) // seg_length
    key_onehot = (key_segment[:, None] == jnp.arange(segments, dtype=jnp.int32)[None, :]).astype(
        jnp.float32
    )
    return (ancestry, marked, key_segment, key_onehot, seg_length)


def block_mask(tables, start_row, block_rows):
    ancestry, marked, key_segment, key_onehot, seg_length = tables
    query_position = start_row + jnp.arange(block_rows, dtype=jnp.int32)
    query_segment = query_position // seg_length
    query_onehot = (
        query_segment[:, None] == jnp.arange(ancestry.shape[0], dtype=jnp.int32)[None, :]
    ).astype(jnp.float32)
    reached = jnp.dot(jnp.dot(query_onehot, ancestry, precision=None), key_onehot.T, precision=None)
    key_position = jnp.arange(marked.shape[0], dtype=jnp.int32)
    same_segment = (query_segment[:, None] == key_segment[None, :]) & (
        key_position[None, :] <= query_position[:, None]
    )
    return same_segment | (reached > 0.5) & (marked[None, :] > 0.5)


def contract(left_side, right_side, left_dim, right_dim):
    return lax.dot_general(
        left_side,
        right_side,
        (((left_dim,), (right_dim,)), ((), ())),
        preferred_element_type=jnp.float32,
    )


def attend_forward(queries, key_states, value_states, tables):
    length = queries.shape[0]
    head_count = queries.shape[1] // HD
    block_rows = min(512, length)
    query_heads = queries.reshape(length, head_count, HD)
    key_heads = key_states.reshape(length, head_count, HD)
    value_heads = value_states.reshape(length, head_count, HD)

    def one_block(start_row):
        query_block = lax.dynamic_slice_in_dim(query_heads, start_row, block_rows, 0)
        scores = jnp.einsum(
            "qhd,khd->hqk", query_block, key_heads, preferred_element_type=jnp.float32
        )
        allowed = block_mask(tables, start_row, block_rows)
        scores = jnp.where(allowed[None], scores, MASKED_SCORE)
        highest = jnp.max(scores, axis=-1, keepdims=True)
        exp_scores = jnp.exp(scores - highest)
        totals = jnp.sum(exp_scores, axis=-1, keepdims=True)
        shares = (exp_scores / totals).astype(jnp.bfloat16)
        attended = jnp.einsum(
            "hqk,khd->qhd", shares, value_heads, preferred_element_type=jnp.float32
        )
        return (attended.astype(jnp.bfloat16), (highest + jnp.log(totals))[..., 0])

    starts = jnp.arange(length // block_rows, dtype=jnp.int32) * block_rows
    attended, log_totals = lax.map(one_block, starts)
    return (attended.reshape(length, head_count * HD), log_totals)


def attend_backward(queries, key_states, value_states, grad_attended, log_totals, tables):
    length = queries.shape[0]
    head_count = queries.shape[1] // HD
    block_rows = min(512, length)
    query_heads = queries.reshape(length, head_count, HD)
    key_heads = key_states.reshape(length, head_count, HD)
    value_heads = value_states.reshape(length, head_count, HD)
    grad_heads = grad_attended.reshape(length, head_count, HD)

    def one_block(summed, members):
        start_row, log_block = members
        key_sum, value_sum = summed
        query_block = lax.dynamic_slice_in_dim(query_heads, start_row, block_rows, 0)
        grad_block = lax.dynamic_slice_in_dim(grad_heads, start_row, block_rows, 0)
        scores = jnp.einsum(
            "qhd,khd->hqk", query_block, key_heads, preferred_element_type=jnp.float32
        )
        allowed = block_mask(tables, start_row, block_rows)
        probs = jnp.where(allowed[None], jnp.exp(scores - log_block[..., None]), 0.0)
        grad_probs = jnp.einsum(
            "qhd,khd->hqk", grad_block, value_heads, preferred_element_type=jnp.float32
        )
        inner_sum = jnp.sum(probs * grad_probs, axis=-1, keepdims=True)
        grad_scores = (probs * (grad_probs - inner_sum)).astype(jnp.bfloat16)
        grad_query = jnp.einsum(
            "hqk,khd->qhd", grad_scores, key_heads, preferred_element_type=jnp.float32
        ).astype(jnp.bfloat16)
        key_sum = key_sum + jnp.einsum(
            "hqk,qhd->khd", grad_scores, query_block, preferred_element_type=jnp.float32
        )
        value_sum = value_sum + jnp.einsum(
            "hqk,qhd->khd",
            probs.astype(jnp.bfloat16),
            grad_block,
            preferred_element_type=jnp.float32,
        )
        return ((key_sum, value_sum), grad_query)

    starts = jnp.arange(length // block_rows, dtype=jnp.int32) * block_rows
    zero_heads = jnp.zeros((length, head_count, HD), jnp.float32)
    (key_sum, value_sum), grad_queries = lax.scan(
        one_block, (zero_heads, zero_heads), (starts, log_totals)
    )
    width = head_count * HD
    return (
        grad_queries.reshape(length, width),
        key_sum.reshape(length, width).astype(jnp.bfloat16),
        value_sum.reshape(length, width).astype(jnp.bfloat16),
    )


def scatter_narrow(partial_sums, axis):
    narrow_sums = lax.psum_scatter(
        partial_sums.astype(jnp.bfloat16), axis, scatter_dimension=0, tiled=True
    )
    return narrow_sums.astype(jnp.float32)


def body(
    tokens,
    norm1_gain,
    norm1_shift,
    w_query,
    b_query,
    w_key,
    w_value,
    b_value,
    w_out,
    b_out,
    norm2_gain,
    norm2_shift,
    w_up,
    b_up,
    w_down,
    b_down,
    teacher,
    valid_mask,
    parents,
    summary,
):

    def attention_weights():
        return (
            lax.all_gather(w_query, "fsdp", axis=0, tiled=True),
            lax.all_gather(w_key, "fsdp", axis=0, tiled=True),
            lax.all_gather(w_value, "fsdp", axis=0, tiled=True),
            lax.all_gather(w_out, "fsdp", axis=0, tiled=True),
        )

    def feed_weights():
        return (
            lax.all_gather(w_up, "fsdp", axis=0, tiled=True),
            lax.all_gather(w_down, "fsdp", axis=0, tiled=True),
        )

    inputs = tokens.astype(jnp.float32)
    normed = layer_norm(inputs, norm1_gain, norm1_shift).astype(jnp.bfloat16)
    normed_all = lax.all_gather(normed, "tp", axis=0, tiled=True)
    full_query, full_key, full_value, full_out = attention_weights()
    queries = (
        (jnp.dot(normed_all, full_query, preferred_element_type=jnp.float32) + b_query) * 0.125
    ).astype(jnp.bfloat16)
    key_states = jnp.dot(normed_all, full_key, preferred_element_type=jnp.float32).astype(
        jnp.bfloat16
    )
    value_states = (
        jnp.dot(normed_all, full_value, preferred_element_type=jnp.float32) + b_value
    ).astype(jnp.bfloat16)
    tables = tree_tables(parents[0], summary[0], normed_all.shape[0])
    attended, log_totals = attend_forward(queries, key_states, value_states, tables)
    branch = scatter_narrow(contract(attended, full_out, 1, 1), "tp")
    hidden = inputs + branch + b_out
    normed_mid = layer_norm(hidden, norm2_gain, norm2_shift).astype(jnp.bfloat16)
    normed_mid_all = lax.all_gather(normed_mid, "tp", axis=0, tiled=True)
    full_up, full_down = feed_weights()
    active = jnp.maximum(
        jnp.dot(normed_mid_all, full_up, preferred_element_type=jnp.float32) + b_up, 0.0
    ).astype(jnp.bfloat16)
    feed_out = scatter_narrow(contract(active, full_down, 1, 1), "tp")
    output = hidden + feed_out + b_down
    weight_mask = valid_mask.astype(jnp.float32)
    deviation = output - teacher.astype(jnp.float32)
    valid_count, squares = lax.psum(
        (jnp.sum(weight_mask), jnp.sum(weight_mask[:, None] * deviation * deviation)),
        ("fsdp", "tp"),
    )
    mean_loss = squares / (valid_count * tokens.shape[1])
    total_tokens = tokens.shape[0] * lax.axis_size("fsdp") * lax.axis_size("tp")
    grad_output = 2.0 * total_tokens / valid_count * weight_mask[:, None] * deviation
    grad_feed_all = lax.all_gather(grad_output.astype(jnp.bfloat16), "tp", axis=0, tiled=True)
    full_up, full_down = feed_weights()
    grad_w_down = contract(grad_feed_all, active, 0, 0)
    grad_pre = jnp.where(
        active > 0, jnp.dot(grad_feed_all, full_down, preferred_element_type=jnp.float32), 0.0
    ).astype(jnp.bfloat16)
    grad_w_up = contract(normed_mid_all, grad_pre, 0, 0)
    grad_w_up, grad_w_down = (
        lax.psum_scatter(
            grad_w_up.astype(jnp.bfloat16), "fsdp", scatter_dimension=0, tiled=True
        ).astype(jnp.float32),
        lax.psum_scatter(
            grad_w_down.astype(jnp.bfloat16), "fsdp", scatter_dimension=0, tiled=True
        ).astype(jnp.float32),
    )
    grad_mid = scatter_narrow(contract(grad_pre, full_up, 1, 1), "tp")
    second_norm, second_pull = jax.vjp(layer_norm, hidden, norm2_gain, norm2_shift)
    grad_hidden_norm, grad_norm2_gain, grad_norm2_shift = second_pull(grad_mid)
    grad_hidden = grad_output + grad_hidden_norm
    grad_branch_all = lax.all_gather(grad_hidden.astype(jnp.bfloat16), "tp", axis=0, tiled=True)
    full_query, full_key, full_value, full_out = attention_weights()
    grad_w_out = contract(grad_branch_all, attended, 0, 0)
    grad_attended = jnp.dot(grad_branch_all, full_out, preferred_element_type=jnp.float32).astype(
        jnp.bfloat16
    )
    grad_queries, grad_keys, grad_values = attend_backward(
        queries, key_states, value_states, grad_attended, log_totals, tables
    )
    grad_pre_query = grad_queries * jnp.bfloat16(0.125)
    grad_w_query = contract(normed_all, grad_pre_query, 0, 0)
    grad_w_key = contract(normed_all, grad_keys, 0, 0)
    grad_w_value = contract(normed_all, grad_values, 0, 0)
    grad_w_query, grad_w_key, grad_w_value, grad_w_out = (
        scatter_narrow(grad_w_query, "fsdp"),
        scatter_narrow(grad_w_key, "fsdp"),
        scatter_narrow(grad_w_value, "fsdp"),
        scatter_narrow(grad_w_out, "fsdp"),
    )
    grad_normed = (
        contract(grad_pre_query, full_query, 1, 1)
        + contract(grad_keys, full_key, 1, 1)
        + contract(grad_values, full_value, 1, 1)
    )
    grad_normed = scatter_narrow(grad_normed, "tp")
    first_norm, first_pull = jax.vjp(layer_norm, inputs, norm1_gain, norm1_shift)
    grad_input_norm, grad_norm1_gain, grad_norm1_shift = first_pull(grad_normed)
    grad_tokens = grad_hidden + grad_input_norm
    column = lax.axis_index("tp")
    tp_count = lax.axis_size("tp")

    def widen(share_part):
        widened = jnp.zeros((share_part.shape[0] * tp_count,), jnp.float32)
        return lax.dynamic_update_slice_in_dim(widened, share_part, column * share_part.shape[0], 0)

    def narrow(widened, span_width):
        return lax.dynamic_slice_in_dim(widened, column * span_width, span_width, 0)

    summed = lax.psum(
        (
            grad_norm1_gain,
            grad_norm1_shift,
            widen(jnp.sum(grad_pre_query.astype(jnp.float32), axis=0)),
            widen(jnp.sum(grad_values.astype(jnp.float32), axis=0)),
            jnp.sum(grad_hidden, axis=0),
            grad_norm2_gain,
            grad_norm2_shift,
            widen(jnp.sum(grad_pre.astype(jnp.float32), axis=0)),
            jnp.sum(grad_output, axis=0),
        ),
        ("fsdp", "tp"),
    )
    return (
        output.astype(jnp.bfloat16),
        mean_loss,
        grad_tokens,
        summed[0],
        summed[1],
        grad_w_query,
        narrow(summed[2], b_query.shape[0]),
        grad_w_key,
        grad_w_value,
        narrow(summed[3], b_value.shape[0]),
        grad_w_out,
        summed[4],
        summed[5],
        summed[6],
        grad_w_up,
        narrow(summed[7], b_up.shape[0]),
        grad_w_down,
        summed[8],
    )


def solution(mesh):
    placed = (
        P(("fsdp", "tp"), None),
        P(),
        P(),
        P("fsdp", "tp"),
        P("tp"),
        P("fsdp", "tp"),
        P("fsdp", "tp"),
        P("tp"),
        P("fsdp", "tp"),
        P(),
        P(),
        P(),
        P("fsdp", "tp"),
        P("tp"),
        P("fsdp", "tp"),
        P(),
        P(("fsdp", "tp"), None),
        P(("fsdp", "tp")),
        P("fsdp", None),
        P("fsdp", None, None),
    )
    return jax.shard_map(
        body,
        mesh=mesh,
        in_specs=placed,
        out_specs=(
            P(("fsdp", "tp"), None),
            P(),
            P(("fsdp", "tp"), None),
            P(),
            P(),
            P("fsdp", "tp"),
            P("tp"),
            P("fsdp", "tp"),
            P("fsdp", "tp"),
            P("tp"),
            P("fsdp", "tp"),
            P(),
            P(),
            P(),
            P("fsdp", "tp"),
            P("tp"),
            P("fsdp", "tp"),
            P(),
        ),
        check_vma=False,
    )
```

profile of v0, /device:TPU:0, one launch (start us, length us, event | category | flops | bytes accessed | tf_op | source)
XLA Modules:
  0.0 1341.5 jit_solution(14886706895732890239)
XLA Ops:
  18.1 22.4 %all-gather.15.cloned.1.call-done = bf16[2048,512]{1,0:T(8,128)(2,1)} async-done(((bf16[256,512]{1,0:T(8,128)(2,1)}), bf16[2048,512]{1,0:T(8,128)(2,1)}) %all-gather.15.cloned.1.call-update) | async-done | bytes 2097168 | tf_op jit(solution)/shard_map/all_gather | solution.py:187
  40.6 82.9 %all-gather.11.cloned.1.call-done = bf16[1024,2048]{1,0:T(8,128)(2,1)} async-done(((bf16[256,2048]{1,0:T(8,128)(2,1)}), bf16[1024,2048]{1,0:T(8,128)(2,1)}) %all-gather.11.cloned.1.call-update) | async-done | bytes 4194320 | tf_op jit(solution)/shard_map/all_gather | solution.py:200
  123.5 5.2 convolution_convert_fusion.11
  128.7 22.9 %all-gather.17.cloned.1.call-done = bf16[2048,512]{1,0:T(8,128)(2,1)} async-done(((bf16[256,512]{1,0:T(8,128)(2,1)}), bf16[2048,512]{1,0:T(8,128)(2,1)}) %all-gather.17.cloned.1.call-update) | async-done | bytes 2097168 | tf_op jit(solution)/shard_map/all_gather | solution.py:188
  151.7 6.2 add_convert_fusion.2
  157.9 23.3 %all-gather.13.cloned.1.call-done = bf16[2048,512]{1,0:T(8,128)(2,1)} async-done(((bf16[256,512]{1,0:T(8,128)(2,1)}), bf16[2048,512]{1,0:T(8,128)(2,1)}) %all-gather.13.cloned.1.call-update) | async-done | bytes 2097168 | tf_op jit(solution)/shard_map/all_gather | solution.py:186
  181.2 5.2 multiply_convert_fusion.1
  187.5 34.3 %while.45 = (s32[]{:T(128)}, bf16[2,512,8,64]{1,3,2,0:T(8,128)(2,1)}, f32[2,8,512]{2,1,0:T(8,128)S(1)}, s32[2]{0:T(128)S(1)}, bf16[8,8]{1,0:T(8,128)(2,1)S(1)}, ...) while((s32[]{:T(128)}, ...), condition=%wide.region_9.10_spmd.clone, body=%wide.region_6.9_spmd.clone.sunk | while | flops 1123386368 | bytes 68315536 | solution.py:99
  192.1 2.9 select_reduce_fusion.2
  195.0 3.8 fusion.178
  198.8 5.0 fusion.179
  209.2 2.9 select_reduce_fusion.2
  212.1 3.8 fusion.178
  215.9 5.0 fusion.179
  221.9 2.7 copy.41
  224.9 6.3 convolution_convert_fusion.5
  232.1 76.1 %reduce-scatter.11.cloned.1.call-done = bf16[256,2048]{1,0:T(8,128)(2,1)} async-done(((bf16[1024,2048]{1,0:T(8,128)(2,1)}), bf16[256,2048]{1,0:T(8,128)(2,1)}) %reduce-scatter.11.cloned.1.call-update) | async-done | bytes 1048592 | tf_op jit(solution)/shard_map/reduce_scatter | solution.py:155
  313.0 51.9 %all-gather.23.cloned.1.call-done = bf16[2048,2048]{1,0:T(8,128)(2,1)} async-done(((bf16[256,2048]{1,0:T(8,128)(2,1)}), bf16[2048,2048]{1,0:T(8,128)(2,1)}) %all-gather.23.cloned.1.call-update) | async-done | bytes 8388624 | tf_op jit(solution)/shard_map/all_gather | solution.py:194
  364.9 82.9 %all-gather.21.cloned.1.call-done = bf16[1024,2048]{1,0:T(8,128)(2,1)} async-done(((bf16[256,2048]{1,0:T(8,128)(2,1)}), bf16[1024,2048]{1,0:T(8,128)(2,1)}) %all-gather.21.cloned.1.call-update) | async-done | bytes 4194320 | tf_op jit(solution)/shard_map/all_gather | solution.py:216
  447.8 14.0 %maximum_convert_fusion = bf16[1024,2048]{1,0:T(8,128)(2,1)} fusion(f32[2048]{0:T(1024)S(1)} %copy-done.46, bf16[1024,2048]{1,0:T(8,128)(2,1)} %all-gather.21.cloned.1.call-done, bf16[2048,2048]{1,0:T(8,128)(2,1)} %all-gather.23.cloned.1.call-done), kind=kOutput, calls=%fused_computation.104 | convolution fusion | flops 8596226048 | bytes 16785408 | tf_op jit(solution)/shard_map/dot_general | solution.py:219
  461.8 40.7 %all-gather.25.cloned.1.call-done = bf16[2048,2048]{1,0:T(8,128)(2,1)} async-done(((bf16[256,2048]{1,0:T(8,128)(2,1)}), bf16[2048,2048]{1,0:T(8,128)(2,1)}) %all-gather.25.cloned.1.call-update) | async-done | bytes 8388624 | tf_op jit(solution)/shard_map/all_gather | solution.py:195
  502.4 13.9 %convolution_convert_fusion.4 = bf16[1024,2048]{1,0:T(8,128)(2,1)} fusion(bf16[1024,2048]{1,0:T(8,128)(2,1)} %maximum_convert_fusion, bf16[2048,2048]{1,0:T(8,128)(2,1)} %all-gather.25.cloned.1.call-done), kind=kOutput, calls=%fused_computation.108 | convolution fusion | flops 8592031744 | bytes 16777216 | tf_op jit(solution)/shard_map/dot_general | solution.py:66
  517.6 44.5 %psum.78 = f32[]{:T(128)} all-reduce(f32[]{:T(128)} %convert_reduce_fusion.7), channel_id=1, replica_groups=mesh['fsdp'=8,'tp'=4] {'fsdp','tp'}, use_global_device_ids=true, to_apply=%region_17.18 | all-reduce | flops 1 | bytes 8 | tf_op jit(solution)/shard_map/psum | solution.py:225
  562.8 31.5 %reduce-scatter.13.cloned.1.call-done = bf16[256,2048]{1,0:T(8,128)(2,1)} async-done(((bf16[1024,2048]{1,0:T(8,128)(2,1)}), bf16[256,2048]{1,0:T(8,128)(2,1)}) %reduce-scatter.13.cloned.1.call-update) | async-done | bytes 1048592 | tf_op jit(solution)/shard_map/reduce_scatter | solution.py:155
  594.4 4.4 multiply_convert_fusion.2
  598.9 81.3 %all-gather.27.cloned.1.call-done = bf16[1024,2048]{1,0:T(8,128)(2,1)} async-done(((bf16[256,2048]{1,0:T(8,128)(2,1)}), bf16[1024,2048]{1,0:T(8,128)(2,1)}) %all-gather.27.cloned.1.call-update) | async-done | bytes 4194320 | tf_op jit(solution)/shard_map/all_gather | solution.py:232
  680.1 14.2 %convert_reduce_fusion = (f32[2048]{0:T(1024)}, bf16[1024,2048]{1,0:T(8,128)(2,1)S(1)}) fusion(bf16[1024,2048]{1,0:T(8,128)(2,1)} %all-gather.27.cloned.1.call-done, bf16[2048,2048]{1,0:T(8,128)(2,1)} %all-gather.25.cloned.1.call-done, bf16[1024,2048]{1,0:T(8,128)(2,1)} %maximum_convert_fusion), kind=kOutput, calls=%fused_computation.101 | convolution fusion | flops 8600418304 | bytes 20979712 | tf_op jit(solution)/shard_map/dot_general | solution.py:236
  696.4 12.6 convolution_convert_fusion.3
  709.0 75.4 %reduce-scatter.15.cloned.1.call-done = bf16[256,2048]{1,0:T(8,128)(2,1)} async-done(((bf16[1024,2048]{1,0:T(8,128)(2,1)}), bf16[256,2048]{1,0:T(8,128)(2,1)}) %reduce-scatter.15.cloned.1.call-update) | async-done | bytes 1048592 | tf_op jit(solution)/shard_map/reduce_scatter | solution.py:155
  784.4 2.8 convert_reduce_fusion.2
  789.0 2.8 fusion.99
  794.2 14.2 %convolution_convert_fusion.1 = bf16[2048,2048]{1,0:T(8,128)(2,1)} fusion(bf16[1024,2048]{1,0:T(8,128)(2,1)} %all-gather.27.cloned.1.call-done, bf16[1024,2048]{1,0:T(8,128)(2,1)} %maximum_convert_fusion), kind=kOutput, calls=%fused_computation.105 | convolution fusion | flops 8594128896 | bytes 16777216 | tf_op jit(solution)/shard_map/dot_general | solution.py:66
  808.5 14.1 %convolution_convert_fusion.2 = bf16[2048,2048]{1,0:T(8,128)(2,1)} fusion(bf16[1024,2048]{1,0:T(8,128)(2,1)} %all-gather.21.cloned.1.call-done, bf16[1024,2048]{1,0:T(8,128)(2,1)} %copy-done.50), kind=kOutput, calls=%fused_computation.106 | convolution fusion | flops 8594128896 | bytes 16777216 | tf_op jit(solution)/shard_map/dot_general | solution.py:66
  822.7 52.9 %all-gather.29.cloned.1.call-done = bf16[1024,2048]{1,0:T(8,128)(2,1)} async-done(((bf16[256,2048]{1,0:T(8,128)(2,1)}), bf16[1024,2048]{1,0:T(8,128)(2,1)}) %all-gather.29.cloned.1.call-update) | async-done | bytes 4194320 | tf_op jit(solution)/shard_map/all_gather | solution.py:251
  875.6 6.2 convolution_convert_fusion.6
  881.9 6.9 convolution_convert_fusion.10
  889.8 105.0 %while.47 = (s32[]{:T(128)}, f32[1024,8,64]{0,2,1:T(8,128)S(1)}, f32[1024,8,64]{0,2,1:T(8,128)}, bf16[2,512,8,64]{1,3,2,0:T(8,128)(2,1)}, s32[2]{0:T(128)S(1)}, ...) while((s32[]{:T(128)}, f32[1024,8,64]{0,2,1:T(8,128)S(1)}, ...), condition=%wide.region_23.24_spmd.clone, body=%wide.region_21.23_spmd.clone.sunk | while | flops 2748679168 | bytes 224012784 | solution.py:143
  895.3 3.6 fusion.194
  898.9 6.2 copy-done
  905.2 5.7 bitcast_add_fusion.5
  910.9 12.9 multiply_reduce_fusion.4
  923.8 12.7 multiply_convert_fusion.4
  936.5 2.7 fusion.196
  946.4 3.6 fusion.194
  950.0 5.7 copy-done
  955.7 6.1 bitcast_add_fusion.5
  961.8 14.7 %multiply_reduce_fusion.4 = (f32[8,512]{1,0:T(8,128)S(1)}, f32[8,512,1024]{2,1,0:T(8,128)}) fusion(f32[8,512,1024]{2,1,0:T(8,128)} %copy-done, f32[8,512]{1,0:T(8,128)S(1)} %dynamic-slice_bitcast_fusion.2, pred[512,1024]{1,0:T(8,128)(4,1)S(1)} %copy-done.4, bf16[1024,8,64]{0,2,1:T(8,128)(2,1)} %get-tuple-element.828, ...), kind=kOutput, calls=%fused_computation.51.clone.1 | convolution fusion | flops 553644032 | bytes 35684356 | tf_op jit(solution)/shard_map/while/body/eval_jaxpr/qhd,khd->hqk/dot_general | solution.py:122
  976.5 13.2 multiply_convert_fusion.4
  989.8 2.7 fusion.196
  997.7 6.1 convolution_convert_fusion.7
  1007.4 3.8 convolution_convert_fusion.9
  1011.4 6.0 convolution_convert_fusion.8
  1017.7 4.2 fusion.101
  1021.9 2.4 fusion.100
  1024.3 6.0 add_convert_fusion
  1031.3 2.9 convert_element_type.217
  1034.3 2.9 convert_element_type.214
  1038.1 30.0 %reduce-scatter.25.cloned.1.call-done = bf16[256,512]{1,0:T(8,128)(2,1)} async-done(((bf16[2048,512]{1,0:T(8,128)(2,1)}), bf16[256,512]{1,0:T(8,128)(2,1)}) %reduce-scatter.25.cloned.1.call-update) | async-done | bytes 262160 | tf_op jit(solution)/shard_map/reduce_scatter | solution.py:155
  1069.9 42.5 %reduce-scatter.23.cloned.1.call-done = bf16[256,512]{1,0:T(8,128)(2,1)} async-done(((bf16[2048,512]{1,0:T(8,128)(2,1)}), bf16[256,512]{1,0:T(8,128)(2,1)}) %reduce-scatter.23.cloned.1.call-update) | async-done | bytes 262160 | tf_op jit(solution)/shard_map/reduce_scatter | solution.py:155
  1114.2 42.5 %reduce-scatter.19.cloned.1.call-done = bf16[256,512]{1,0:T(8,128)(2,1)} async-done(((bf16[2048,512]{1,0:T(8,128)(2,1)}), bf16[256,512]{1,0:T(8,128)(2,1)}) %reduce-scatter.19.cloned.1.call-update) | async-done | bytes 262160 | tf_op jit(solution)/shard_map/reduce_scatter | solution.py:155
  1158.4 42.6 %reduce-scatter.21.cloned.1.call-done = bf16[256,512]{1,0:T(8,128)(2,1)} async-done(((bf16[2048,512]{1,0:T(8,128)(2,1)}), bf16[256,512]{1,0:T(8,128)(2,1)}) %reduce-scatter.21.cloned.1.call-update) | async-done | bytes 262160 | tf_op jit(solution)/shard_map/reduce_scatter | solution.py:155
  1202.9 77.1 %reduce-scatter.17.cloned.1.call-done = bf16[256,2048]{1,0:T(8,128)(2,1)} async-done(((bf16[1024,2048]{1,0:T(8,128)(2,1)}), bf16[256,2048]{1,0:T(8,128)(2,1)}) %reduce-scatter.17.cloned.1.call-update) | async-done | bytes 1048592 | tf_op jit(solution)/shard_map/reduce_scatter | solution.py:155
  1284.3 43.1 %all-reduce.2 = (f32[]{:T(128)}, f32[2048]{0:T(1024)}, f32[2048]{0:T(1024)}, f32[2048]{0:T(1024)S(1)}, f32[2048]{0:T(1024)S(1)}, /*index=5*/f32[2048]{0:T(1024)}...) all-reduce(f32[]{:T(128)} %get-tuple-element.543, ...), channel_id=1, replica_groups=mesh['fsdp'=8,'tp'=4] {'fsdp','tp'}, use_global_device_ids=true, to_apply=%region_15.16 | all-reduce | flops 24577 | bytes 196616 | tf_op jit(solution)/shard_map/psum | solution.py:225
  1330.0 3.3 add_add_fusion.2
  (264 shorter events, 67.4 us)
Async XLA Ops:
  7.2 5.1 copy-start.1
  7.2 5.1 copy-start.25
  7.2 5.1 copy-start.38
  7.2 33.3 %all-gather.15.cloned.1.call-start = ((), (), s32[]{:S(2)}) async-start(), calls=%async_computation.12 | async-start | bytes 2359296 | tf_op jit(solution)/shard_map/all_gather | solution.py:187
  8.0 115.5 %all-gather.11.cloned.1.call-start = ((), (), s32[]{:S(2)}) async-start(), calls=%async_computation.10 | async-start | bytes 5242880 | tf_op jit(solution)/shard_map/all_gather | solution.py:200
  9.5 2.2 copy-start.28
  11.7 4.0 copy-start.49
  11.7 6.3 copy-start.42
  13.7 137.9 %all-gather.17.cloned.1.call-start = ((), (), s32[]{:S(2)}) async-start(), calls=%async_computation.13 | async-start | bytes 2359296 | tf_op jit(solution)/shard_map/all_gather | solution.py:188
  14.5 166.8 %all-gather.13.cloned.1.call-start = ((), (), s32[]{:S(2)}) async-start(), calls=%async_computation.11 | async-start | bytes 2359296 | tf_op jit(solution)/shard_map/all_gather | solution.py:186
  15.0 209.8 %all-gather.19.cloned.1.call-start = ((), (), s32[]{:S(2)}) async-start(), calls=%async_computation.14 | async-start | bytes 2359296 | tf_op jit(solution)/shard_map/all_gather | solution.py:189
  15.6 292.6 %reduce-scatter.11.cloned.1.call-start = ((), (), s32[]{:S(2)}) async-start(), calls=%async_computation.15 | async-start | bytes 5242880 | tf_op jit(solution)/shard_map/reduce_scatter | solution.py:155
  18.1 133.5 %copy-start.47 = (f32[512]{0:T(512)S(1)}, f32[512]{0:T(512)}, u32[]{:S(2)}) copy-start(f32[512]{0:T(512)} %param.33) | copy-start | bytes 6148
  128.7 52.5 %copy-start.48 = (f32[512]{0:T(512)S(1)}, f32[512]{0:T(512)}, u32[]{:S(2)}) copy-start(f32[512]{0:T(512)} %param.30) | copy-start | bytes 6148
  195.0 3.8 copy-start.8
  195.0 3.8 copy-start.19
  212.1 3.8 copy-start.8
  212.1 3.8 copy-start.19
  221.9 9.3 copy-start.5
  224.8 6.4 copy-start.21
  231.2 77.0 %copy-start.2 = (bf16[256,2048]{1,0:T(8,128)(2,1)S(1)}, bf16[256,2048]{1,0:T(8,128)(2,1)}, u32[]{:S(2)}) copy-start(bf16[256,2048]{1,0:T(8,128)(2,1)} %param.26) | copy-start | bytes 3145732
  231.2 77.0 %copy-start.24 = (f32[2048]{0:T(1024)S(1)}, f32[2048]{0:T(1024)}, u32[]{:S(2)}) copy-start(f32[2048]{0:T(1024)} %param.35) | copy-start | bytes 24580
  231.2 133.6 %all-gather.23.cloned.1.call-start = ((), (), s32[]{:S(2)}) async-start(), calls=%async_computation.17 | async-start | bytes 9437184 | tf_op jit(solution)/shard_map/all_gather | solution.py:194
  232.0 78.5 %copy-start.27 = (f32[2048]{0:T(1024)S(1)}, f32[2048]{0:T(1024)}, u32[]{:S(2)}) copy-start(f32[2048]{0:T(1024)} %param.36) | copy-start | bytes 24580
  232.0 78.5 %copy-start.39 = (f32[2048]{0:T(1024)S(1)}, f32[2048]{0:T(1024)}, u32[]{:S(2)}) copy-start(f32[2048]{0:T(1024)} %param.37) | copy-start | bytes 24580
  232.0 215.8 %all-gather.21.cloned.1.call-start = ((), (), s32[]{:S(2)}) async-start(), calls=%async_computation.16 | async-start | bytes 5242880 | tf_op jit(solution)/shard_map/all_gather | solution.py:216
  310.5 137.2 %copy-start.46 = (f32[2048]{0:T(1024)S(1)}, f32[2048]{0:T(1024)}, u32[]{:S(2)}) copy-start(f32[2048]{0:T(1024)} %param.39) | copy-start | bytes 24580
  312.2 190.2 %all-gather.25.cloned.1.call-start = ((), (), s32[]{:S(2)}) async-start(), calls=%async_computation.18 | async-start | bytes 9437184 | tf_op jit(solution)/shard_map/all_gather | solution.py:195
  313.0 281.4 %reduce-scatter.13.cloned.1.call-start = ((), (), s32[]{:S(2)}) async-start(), calls=%async_computation.19 | async-start | bytes 5242880 | tf_op jit(solution)/shard_map/reduce_scatter | solution.py:155
  516.4 78.0 %copy-start.41 = (f32[2048]{0:T(1024)S(1)}, f32[2048]{0:T(1024)}, u32[]{:S(2)}) copy-start(f32[2048]{0:T(1024)} %param.41) | copy-start | bytes 24580
  516.4 163.8 %all-gather.27.cloned.1.call-start = ((), (), s32[]{:S(2)}) async-start(), calls=%async_computation.20 | async-start | bytes 5242880 | tf_op jit(solution)/shard_map/all_gather | solution.py:232
  598.8 185.6 %reduce-scatter.15.cloned.1.call-start = ((), (), s32[]{:S(2)}) async-start(), calls=%async_computation.21 | async-start | bytes 5242880 | tf_op jit(solution)/shard_map/reduce_scatter | solution.py:155
  709.0 166.6 %all-gather.29.cloned.1.call-start = ((), (), s32[]{:S(2)}) async-start(), calls=%async_computation.22 | async-start | bytes 5242880 | tf_op jit(solution)/shard_map/all_gather | solution.py:251
  784.4 2.8 copy-start.15
  794.2 237.2 %reduce-scatter.29.cloned.1.call-start = ((), (), s32[]{:S(2)}) async-start(), calls=%async_computation.29 | async-start | bytes 9437184 | tf_op jit(solution)/shard_map/reduce_scatter | solution.py:243
  808.5 225.8 %reduce-scatter.27.cloned.1.call-start = ((), (), s32[]{:S(2)}) async-start(), calls=%async_computation.28 | async-start | bytes 9437184 | tf_op jit(solution)/shard_map/reduce_scatter | solution.py:240
  822.6 245.5 %reduce-scatter.25.cloned.1.call-start = ((), (), s32[]{:S(2)}) async-start(), calls=%async_computation.27 | async-start | bytes 2359296 | tf_op jit(solution)/shard_map/reduce_scatter | solution.py:155
  881.8 230.5 %reduce-scatter.23.cloned.1.call-start = ((), (), s32[]{:S(2)}) async-start(), calls=%async_computation.26 | async-start | bytes 2359296 | tf_op jit(solution)/shard_map/reduce_scatter | solution.py:155
  895.3 9.9 copy-start.4
  898.9 6.2 copy-start
  923.8 12.7 copy-start.11
  936.5 2.7 copy-start.6
  946.4 9.3 copy-start.4
  950.0 5.7 copy-start
  976.5 13.3 copy-start.11
  989.8 2.7 copy-start.6
  1003.7 152.9 %reduce-scatter.19.cloned.1.call-start = ((), (), s32[]{:S(2)}) async-start(), calls=%async_computation.24 | async-start | bytes 2359296 | tf_op jit(solution)/shard_map/reduce_scatter | solution.py:155
  1005.0 2.3 copy-start.44
  1011.2 189.9 %reduce-scatter.21.cloned.1.call-start = ((), (), s32[]{:S(2)}) async-start(), calls=%async_computation.25 | async-start | bytes 2359296 | tf_op jit(solution)/shard_map/reduce_scatter | solution.py:155
  1017.4 4.4 copy-start.23
  1017.4 262.6 %reduce-scatter.17.cloned.1.call-start = ((), (), s32[]{:S(2)}) async-start(), calls=%async_computation.23 | async-start | bytes 5242880 | tf_op jit(solution)/shard_map/reduce_scatter | solution.py:155
  1017.7 4.2 copy-start.45
  1021.9 2.4 copy-start.18
  1034.3 2.9 copy-start.14
  1037.2 242.9 %copy-start.3 = (bf16[256,2048]{1,0:T(8,128)(2,1)S(1)}, bf16[256,2048]{1,0:T(8,128)(2,1)}, u32[]{:S(2)}) copy-start(bf16[256,2048]{1,0:T(8,128)(2,1)} %param.26) | copy-start | bytes 3145732
  1037.2 242.9 %copy-start.26 = (f32[2048]{0:T(1024)S(1)}, f32[2048]{0:T(1024)}, u32[]{:S(2)}) copy-start(f32[2048]{0:T(1024)} %param.27) | copy-start | bytes 24580
  1037.2 242.9 %copy-start.29 = (f32[256]{0:T(256)S(1)}, f32[256]{0:T(256)}, u32[]{:S(2)}) copy-start(f32[256]{0:T(256)} %copy-done.28) | copy-start | bytes 3076
  1069.9 212.1 %copy-start.37 = (f32[256]{0:T(256)S(1)}, f32[256]{0:T(256)}, u32[]{:S(2)}) copy-start(f32[256]{0:T(256)} %copy-done.36) | copy-start | bytes 3076
  1069.9 212.1 %copy-start.35 = (f32[256]{0:T(256)S(1)}, f32[256]{0:T(256)}, u32[]{:S(2)}) copy-start(f32[256]{0:T(256)} %copy-done.34) | copy-start | bytes 3076
  1202.9 81.4 %copy-start.30 = (f32[2048]{0:T(1024)S(1)}, f32[2048]{0:T(1024)}, u32[]{:S(2)}) copy-start(f32[2048]{0:T(1024)} %get-tuple-element.460) | copy-start | bytes 24580
  1202.9 81.4 %copy-start.31 = (f32[2048]{0:T(1024)S(1)}, f32[2048]{0:T(1024)}, u32[]{:S(2)}) copy-start(f32[2048]{0:T(1024)} %get-tuple-element.454) | copy-start | bytes 24580
  1202.9 81.4 %copy-start.32 = (f32[2048]{0:T(1024)S(1)}, f32[2048]{0:T(1024)}, u32[]{:S(2)}) copy-start(f32[2048]{0:T(1024)} %get-tuple-element.528) | copy-start | bytes 24580
  1202.9 81.4 %copy-start.33 = (f32[2048]{0:T(1024)S(1)}, f32[2048]{0:T(1024)}, u32[]{:S(2)}) copy-start(f32[2048]{0:T(1024)} %get-tuple-element.544) | copy-start | bytes 24580
  1202.9 127.1 %copy-start.10 = (f32[256,2048]{1,0:T(8,128)S(1)}, f32[256,2048]{1,0:T(8,128)}, u32[]{:S(2)}) copy-start(f32[256,2048]{1,0:T(8,128)} %copy-done.9) | copy-start | bytes 6291460
  (15 other events, 18.3 us)
Sparse Core Ops, SparseCore 0:
  9.9 30.5 all-gather.14
  42.7 80.7 all-gather.10
  125.4 26.2 all-gather.16
  153.4 27.7 all-gather.12
  183.0 27.7 all-gather.18
  231.4 76.7 reduce-scatter.10
  310.1 54.7 all-gather.22
  367.0 80.7 all-gather.20
  449.7 52.7 all-gather.24
  516.5 77.8 reduce-scatter.12
  598.9 81.1 all-gather.26
  709.1 75.2 reduce-scatter.14
  794.3 81.2 all-gather.28
  878.9 69.9 reduce-scatter.28
  952.2 71.5 reduce-scatter.26
  1026.9 41.1 reduce-scatter.24
  1071.2 41.1 reduce-scatter.22
  1115.5 41.1 reduce-scatter.18
  1159.9 41.1 reduce-scatter.20
  1203.2 76.7 reduce-scatter.16
where the time goes:
time: 1350 us; the launch traced here: 1340 us
  waiting for transfers between devices  883 us (65%)
  matrix products  225 us (17%)
  blocking collectives  87.6 us (6%)
  other arithmetic  83.4 us (6%)
  local copies, waits for them, and re-layouts  33.8 us (3%)
  between operations  18.2 us (1%)
    reduce_scatter x8, waiting for transfers between devices, scatter_narrow(): lax.psum_scatter(partial_sums.astype(jnp.bfloat16), axis, scatter_dimensi...  418 us
    dot_general x12, matrix products, contract(): lax.dot_general(left_side, right_side, (((left_dim,), (right_dim,)), ((),...  95.7 us
    psum x2, blocking collectives, body(): lax.psum((jnp.sum(weight_mask), jnp.sum(weight_mask[:, None] * deviation...  87.6 us
    all_gather x1, waiting for transfers between devices, body(): normed_all = lax.all_gather(normed, 'tp', axis=0, tiled=True)  82.9 us
    all_gather x1, waiting for transfers between devices, body(): normed_mid_all = lax.all_gather(normed_mid, 'tp', axis=0, tiled=True)  82.9 us
    all_gather x1, waiting for transfers between devices, body(): lax.all_gather(grad_output.astype(jnp.bfloat16), 'tp', axis=0, tiled=True)  81.3 us
    all_gather x1, waiting for transfers between devices, body(): lax.all_gather(grad_hidden.astype(jnp.bfloat16), 'tp', axis=0, tiled=True)  52.9 us
    all_gather x1, waiting for transfers between devices, feed_weights(): lax.all_gather(w_up, 'fsdp', axis=0, tiled=True)  51.9 us
  transfers between devices with their start and end apart: 20, of which 17 were waited for; matrix products, arithmetic and copies ran while one was open for 19% of the time, Pallas kernels for 0%

commit v1 on v0

--- a/solution.py
+++ b/solution.py
@@ -6,6 +6,18 @@
 HD = 64
 EPSILON = 1e-05
 MASKED_SCORE = -1e30
+
+
+def gather_around(array, axis, dim):
+    ways, here, step = (lax.axis_size(axis), lax.axis_index(axis), array.shape[dim])
+    dims = [n * ways if d == dim else n for d, n in enumerate(array.shape)]
+    full = lax.dynamic_update_slice_in_dim(
+        jnp.zeros(dims, array.dtype), array, here * step, axis=dim
+    )
+    for far in range(1, ways):
+        array = lax.ppermute(array, axis, [(d, (d + 1) % ways) for d in range(ways)])
+        full = lax.dynamic_update_slice_in_dim(full, array, (here - far) % ways * step, axis=dim)
+    return full
 
 
 def layer_norm(vectors, norm_gain, norm_shift):
@@ -190,10 +202,7 @@
         )
 
     def feed_weights():
-        return (
-            lax.all_gather(w_up, "fsdp", axis=0, tiled=True),
-            lax.all_gather(w_down, "fsdp", axis=0, tiled=True),
-        )
+        return (lax.all_gather(w_up, "fsdp", axis=0, tiled=True), gather_around(w_down, "fsdp", 0))
 
     inputs = tokens.astype(jnp.float32)
     normed = layer_norm(inputs, norm1_gain, norm1_shift).astype(jnp.bfloat16)

time: 1350 us -> 1320 us (0.978)
  waiting for transfers between devices: 883 us -> 835 us
  local copies, waits for them, and re-layouts: 33.8 us -> 56.5 us
    ppermute x0 -> x7, waiting for transfers between devices: none -> 103 us  [gather_around(): lax.ppermute(array, axis, [(d, (d + 1) % ways) for d in range(ways)])]
    all_gather x1, waiting for transfers between devices: 51.9 us -> 0.01 us  [feed_weights(): lax.all_gather(w_up, 'fsdp', axis=0, tiled=True)]
    all_gather x1, waiting for transfers between devices: 82.9 us -> 41.4 us  [body(): normed_mid_all = lax.all_gather(normed_mid, 'tp', axis=0, tiled=True)]
    all_gather x1 -> x0, waiting for transfers between devices: 40.7 us -> none  [feed_weights(): lax.all_gather(w_down, 'fsdp', axis=0, tiled=True)]
    reduce_scatter x8, waiting for transfers between devices: 418 us -> 402 us  [scatter_narrow(): lax.psum_scatter(partial_sums.astype(jnp.bfloat16), axis, scatter_dimensi...]
    dynamic_update_slice x0 -> x8, local copies, waits for them, and re-layouts: none -> 13.6 us  [the longest x7 12.5 us: gather_around(): lax.dynamic_update_slice_in_dim(full, array, (here - far) % ways * step,...]
  transfers between devices with their start and end apart: 20 -> 26, of which waited for: 17 -> 21; matrix products, arithmetic and copies ran while one was open for 19% -> 19% of each run, Pallas kernels for 0% -> 0%
where the time goes in v1:
time: 1320 us; the launch traced here: 1310 us
  waiting for transfers between devices  835 us (63%)
  matrix products  222 us (17%)
  blocking collectives  86.9 us (7%)
  other arithmetic  82.9 us (6%)
  local copies, waits for them, and re-layouts  56.5 us (4%)
  between operations  18.3 us (1%)
    reduce_scatter x8, waiting for transfers between devices, scatter_narrow(): lax.psum_scatter(partial_sums.astype(jnp.bfloat16), axis, scatter_dimensi...  402 us
    ppermute x7, waiting for transfers between devices, gather_around(): lax.ppermute(array, axis, [(d, (d + 1) % ways) for d in range(ways)])  103 us
    dot_general x12, matrix products, contract(): lax.dot_general(left_side, right_side, (((left_dim,), (right_dim,)), ((),...  94.3 us
    psum x2, blocking collectives, body(): lax.psum((jnp.sum(weight_mask), jnp.sum(weight_mask[:, None] * deviation...  86.9 us
    all_gather x1, waiting for transfers between devices, body(): normed_all = lax.all_gather(normed, 'tp', axis=0, tiled=True)  82.9 us
    all_gather x1, waiting for transfers between devices, body(): lax.all_gather(grad_output.astype(jnp.bfloat16), 'tp', axis=0, tiled=True)  81.1 us
    all_gather x1, waiting for transfers between devices, body(): lax.all_gather(grad_hidden.astype(jnp.bfloat16), 'tp', axis=0, tiled=True)  52.6 us
    all_gather x1, waiting for transfers between devices, body(): normed_mid_all = lax.all_gather(normed_mid, 'tp', axis=0, tiled=True)  41.4 us
  transfers between devices with their start and end apart: 26, of which 21 were waited for; matrix products, arithmetic and copies ran while one was open for 19% of the time, Pallas kernels for 0%

profile of v1, /device:TPU:0, one launch (start us, length us, event | category | flops | bytes accessed | tf_op | source)
XLA Modules:
  0.0 1313.1 jit_solution(14491920027160919450)
XLA Ops:
  18.1 22.4 %all-gather.14.cloned.1.call-done = bf16[2048,512]{1,0:T(8,128)(2,1)} async-done(((bf16[256,512]{1,0:T(8,128)(2,1)}), bf16[2048,512]{1,0:T(8,128)(2,1)}) %all-gather.14.cloned.1.call-update) | async-done | bytes 2097168 | tf_op jit(solution)/shard_map/all_gather | solution.py:199
  40.6 82.9 %all-gather.10.cloned.1.call-done = bf16[1024,2048]{1,0:T(8,128)(2,1)} async-done(((bf16[256,2048]{1,0:T(8,128)(2,1)}), bf16[1024,2048]{1,0:T(8,128)(2,1)}) %all-gather.10.cloned.1.call-update) | async-done | bytes 4194320 | tf_op jit(solution)/shard_map/all_gather | solution.py:209
  123.5 5.2 convolution_convert_fusion.11
  128.7 22.9 %all-gather.16.cloned.1.call-done = bf16[2048,512]{1,0:T(8,128)(2,1)} async-done(((bf16[256,512]{1,0:T(8,128)(2,1)}), bf16[2048,512]{1,0:T(8,128)(2,1)}) %all-gather.16.cloned.1.call-update) | async-done | bytes 2097168 | tf_op jit(solution)/shard_map/all_gather | solution.py:200
  151.7 6.2 add_convert_fusion.2
  157.9 23.3 %all-gather.12.cloned.1.call-done = bf16[2048,512]{1,0:T(8,128)(2,1)} async-done(((bf16[256,512]{1,0:T(8,128)(2,1)}), bf16[2048,512]{1,0:T(8,128)(2,1)}) %all-gather.12.cloned.1.call-update) | async-done | bytes 2097168 | tf_op jit(solution)/shard_map/all_gather | solution.py:198
  181.2 5.2 multiply_convert_fusion.1
  187.5 34.4 %while.45 = (s32[]{:T(128)}, bf16[2,512,8,64]{1,3,2,0:T(8,128)(2,1)}, f32[2,8,512]{2,1,0:T(8,128)S(1)}, s32[2]{0:T(128)S(1)}, bf16[8,8]{1,0:T(8,128)(2,1)S(1)}, ...) while((s32[]{:T(128)}, ...), condition=%wide.region_9.10_spmd.clone, body=%wide.region_6.9_spmd.clone.sunk | while | flops 1123386368 | bytes 68315536 | solution.py:111
  192.2 2.9 select_reduce_fusion.2
  195.1 3.8 fusion.178
  198.9 5.0 fusion.179
  209.3 2.9 select_reduce_fusion.2
  212.2 3.8 fusion.178
  216.0 5.0 fusion.179
  222.0 3.1 copy.41
  225.4 6.4 convolution_convert_fusion.5
  233.2 15.0 %collective-permute-done = bf16[256,2048]{1,0:T(8,128)(2,1)} collective-permute-done((bf16[256,2048]{1,0:T(8,128)(2,1)S(1)}, bf16[256,2048]{1,0:T(8,128)(2,1)}, u32[]{:S(2)}, u32[]{:S(2)}) %collective-permute-start) | collective-permute-done | bytes 1048608 | tf_op jit(solution)/shard_map/ppermute | solution.py:18
  248.2 60.5 %reduce-scatter.11.cloned.1.call-done = bf16[256,2048]{1,0:T(8,128)(2,1)} async-done(((bf16[1024,2048]{1,0:T(8,128)(2,1)}), bf16[256,2048]{1,0:T(8,128)(2,1)}) %reduce-scatter.11.cloned.1.call-update) | async-done | bytes 1048592 | tf_op jit(solution)/shard_map/reduce_scatter | solution.py:167
  313.3 26.6 %collective-permute-done.2 = bf16[256,2048]{1,0:T(8,128)(2,1)S(1)} collective-permute-done((bf16[256,2048]{1,0:T(8,128)(2,1)}, bf16[256,2048]{1,0:T(8,128)(2,1)S(1)}, u32[]{:S(2)}, u32[]{:S(2)}) %collective-permute-start.2) | collective-permute-done | bytes 1048608 | tf_op jit(solution)/shard_map/ppermute | solution.py:18
  340.8 32.6 %collective-permute-done.3 = bf16[256,2048]{1,0:T(8,128)(2,1)S(1)} collective-permute-done((bf16[256,2048]{1,0:T(8,128)(2,1)S(1)}, bf16[256,2048]{1,0:T(8,128)(2,1)S(1)}, u32[]{:S(2)}, u32[]{:S(2)}) %collective-permute-start.3) | collective-permute-done | bytes 1048608 | tf_op jit(solution)/shard_map/ppermute | solution.py:18
  374.4 15.4 %collective-permute-done.4 = bf16[256,2048]{1,0:T(8,128)(2,1)} collective-permute-done((bf16[256,2048]{1,0:T(8,128)(2,1)S(1)}, bf16[256,2048]{1,0:T(8,128)(2,1)}, u32[]{:S(2)}, u32[]{:S(2)}) %collective-permute-start.4) | collective-permute-done | bytes 1048608 | tf_op jit(solution)/shard_map/ppermute | solution.py:18
  389.8 4.3 broadcast.327
  397.5 7.7 collective-permute-done.5
  414.3 6.3 collective-permute-done.6
  421.6 41.4 %all-gather.20.cloned.1.call-done = bf16[1024,2048]{1,0:T(8,128)(2,1)} async-done(((bf16[256,2048]{1,0:T(8,128)(2,1)}), bf16[1024,2048]{1,0:T(8,128)(2,1)}) %all-gather.20.cloned.1.call-update) | async-done | bytes 4194320 | tf_op jit(solution)/shard_map/all_gather | solution.py:225
  462.9 12.5 maximum_convert_fusion
  477.4 12.6 convolution_convert_fusion.4
  491.3 43.7 %psum.78 = f32[]{:T(128)} all-reduce(f32[]{:T(128)} %convert_reduce_fusion.7), channel_id=1, replica_groups=mesh['fsdp'=8,'tp'=4] {'fsdp','tp'}, use_global_device_ids=true, to_apply=%region_17.18 | all-reduce | flops 1 | bytes 8 | tf_op jit(solution)/shard_map/psum | solution.py:234
  535.8 30.8 %reduce-scatter.13.cloned.1.call-done = bf16[256,2048]{1,0:T(8,128)(2,1)} async-done(((bf16[1024,2048]{1,0:T(8,128)(2,1)}), bf16[256,2048]{1,0:T(8,128)(2,1)}) %reduce-scatter.13.cloned.1.call-update) | async-done | bytes 1048592 | tf_op jit(solution)/shard_map/reduce_scatter | solution.py:167
  566.6 4.1 multiply_convert_fusion.2
  570.9 81.1 %all-gather.24.cloned.1.call-done = bf16[1024,2048]{1,0:T(8,128)(2,1)} async-done(((bf16[256,2048]{1,0:T(8,128)(2,1)}), bf16[1024,2048]{1,0:T(8,128)(2,1)}) %all-gather.24.cloned.1.call-update) | async-done | bytes 4194320 | tf_op jit(solution)/shard_map/all_gather | solution.py:241
  652.0 13.8 %convert_reduce_fusion = (f32[2048]{0:T(1024)}, bf16[1024,2048]{1,0:T(8,128)(2,1)S(1)}) fusion(bf16[1024,2048]{1,0:T(8,128)(2,1)} %all-gather.24.cloned.1.call-done, bf16[2048,2048]{1,0:T(8,128)(2,1)} %constant_dynamic-update-slice_fusion, bf16[1024,2048]{1,0:T(8,128)(2,1)} %copy-done.69), kind=kOutput, calls=%fused_computation.101 | convolution fusion | flops 8600418304 | bytes 20979712 | tf_op jit(solution)/shard_map/dot_general | solution.py:245
  667.8 12.6 convolution_convert_fusion.3
  680.5 75.4 %reduce-scatter.15.cloned.1.call-done = bf16[256,2048]{1,0:T(8,128)(2,1)} async-done(((bf16[1024,2048]{1,0:T(8,128)(2,1)}), bf16[256,2048]{1,0:T(8,128)(2,1)}) %reduce-scatter.15.cloned.1.call-update) | async-done | bytes 1048592 | tf_op jit(solution)/shard_map/reduce_scatter | solution.py:167
  766.2 14.1 %convolution_convert_fusion.1 = bf16[2048,2048]{1,0:T(8,128)(2,1)} fusion(bf16[1024,2048]{1,0:T(8,128)(2,1)} %all-gather.24.cloned.1.call-done, bf16[1024,2048]{1,0:T(8,128)(2,1)} %copy-done.69), kind=kOutput, calls=%fused_computation.105 | convolution fusion | flops 8594128896 | bytes 16777216 | tf_op jit(solution)/shard_map/dot_general | solution.py:78
  780.3 14.1 %convolution_convert_fusion.2 = bf16[2048,2048]{1,0:T(8,128)(2,1)} fusion(bf16[1024,2048]{1,0:T(8,128)(2,1)} %all-gather.20.cloned.1.call-done, bf16[1024,2048]{1,0:T(8,128)(2,1)} %copy-done.70), kind=kOutput, calls=%fused_computation.106 | convolution fusion | flops 8594128896 | bytes 16777216 | tf_op jit(solution)/shard_map/dot_general | solution.py:78
  794.5 52.6 %all-gather.26.cloned.1.call-done = bf16[1024,2048]{1,0:T(8,128)(2,1)} async-done(((bf16[256,2048]{1,0:T(8,128)(2,1)}), bf16[1024,2048]{1,0:T(8,128)(2,1)}) %all-gather.26.cloned.1.call-update) | async-done | bytes 4194320 | tf_op jit(solution)/shard_map/all_gather | solution.py:260
  847.1 5.9 convolution_convert_fusion.6
  853.2 7.0 convolution_convert_fusion.10
  861.3 104.8 %while.47 = (s32[]{:T(128)}, f32[1024,8,64]{0,2,1:T(8,128)S(1)}, f32[1024,8,64]{0,2,1:T(8,128)}, bf16[2,512,8,64]{1,3,2,0:T(8,128)(2,1)}, s32[2]{0:T(128)S(1)}, ...) while((s32[]{:T(128)}, f32[1024,8,64]{0,2,1:T(8,128)S(1)}, ...), condition=%wide.region_23.24_spmd.clone, body=%wide.region_21.23_spmd.clone.sunk | while | flops 2748679168 | bytes 224012784 | solution.py:155
  866.8 3.6 fusion.194
  870.4 6.2 copy-done
  876.6 5.7 bitcast_add_fusion.5
  882.3 13.0 multiply_reduce_fusion.4
  895.3 12.6 multiply_convert_fusion.4
  917.8 3.6 fusion.194
  921.4 5.7 copy-done
  927.1 6.1 bitcast_add_fusion.5
  933.2 14.9 %multiply_reduce_fusion.4 = (f32[8,512]{1,0:T(8,128)S(1)}, f32[8,512,1024]{2,1,0:T(8,128)}) fusion(f32[8,512,1024]{2,1,0:T(8,128)} %copy-done, f32[8,512]{1,0:T(8,128)S(1)} %dynamic-slice_bitcast_fusion.2, pred[512,1024]{1,0:T(8,128)(4,1)S(1)} %copy-done.6, bf16[1024,8,64]{0,2,1:T(8,128)(2,1)} %get-tuple-element.828, ...), kind=kOutput, calls=%fused_computation.51.clone.1 | convolution fusion | flops 553644032 | bytes 35684356 | tf_op jit(solution)/shard_map/while/body/eval_jaxpr/qhd,khd->hqk/dot_general | solution.py:134
  948.0 13.2 %multiply_convert_fusion.4 = bf16[8,512,1024]{2,1,0:T(8,128)(2,1)S(1)} fusion(f32[8,512,1024]{2,1,0:T(8,128)} %get-tuple-element.726, f32[8,512,1024]{2,1,0:T(8,128)} %copy-done, f32[8,512]{1,0:T(8,128)S(1)} %get-tuple-element.727, f32[8,512]{1,0:T(8,128)S(1)} %dynamic-slice_bitcast_fusion.2, pred[512,1024]{1,0:T(8,128)(4,1)S(1)} %copy-done.6), kind=kLoop, calls=%fused_computation.50.clone.1 | loop fusion | flops 20971520 | bytes 42500096 | tf_op jit(solution)/shard_map/while/body/eval_jaxpr/convert_element_type | solution.py:138
  969.0 6.1 convolution_convert_fusion.7
  978.7 3.9 convolution_convert_fusion.9
  982.8 6.0 convolution_convert_fusion.8
  989.2 4.2 fusion.101
  995.8 6.0 add_convert_fusion
  1002.9 2.9 convert_element_type.217
  1005.8 2.9 convert_element_type.214
  1009.6 30.2 %reduce-scatter.25.cloned.1.call-done = bf16[256,512]{1,0:T(8,128)(2,1)} async-done(((bf16[2048,512]{1,0:T(8,128)(2,1)}), bf16[256,512]{1,0:T(8,128)(2,1)}) %reduce-scatter.25.cloned.1.call-update) | async-done | bytes 262160 | tf_op jit(solution)/shard_map/reduce_scatter | solution.py:167
  1041.6 42.5 %reduce-scatter.23.cloned.1.call-done = bf16[256,512]{1,0:T(8,128)(2,1)} async-done(((bf16[2048,512]{1,0:T(8,128)(2,1)}), bf16[256,512]{1,0:T(8,128)(2,1)}) %reduce-scatter.23.cloned.1.call-update) | async-done | bytes 262160 | tf_op jit(solution)/shard_map/reduce_scatter | solution.py:167
  1085.9 42.5 %reduce-scatter.19.cloned.1.call-done = bf16[256,512]{1,0:T(8,128)(2,1)} async-done(((bf16[2048,512]{1,0:T(8,128)(2,1)}), bf16[256,512]{1,0:T(8,128)(2,1)}) %reduce-scatter.19.cloned.1.call-update) | async-done | bytes 262160 | tf_op jit(solution)/shard_map/reduce_scatter | solution.py:167
  1130.2 42.5 %reduce-scatter.21.cloned.1.call-done = bf16[256,512]{1,0:T(8,128)(2,1)} async-done(((bf16[2048,512]{1,0:T(8,128)(2,1)}), bf16[256,512]{1,0:T(8,128)(2,1)}) %reduce-scatter.21.cloned.1.call-update) | async-done | bytes 262160 | tf_op jit(solution)/shard_map/reduce_scatter | solution.py:167
  1174.5 77.3 %reduce-scatter.17.cloned.1.call-done = bf16[256,2048]{1,0:T(8,128)(2,1)} async-done(((bf16[1024,2048]{1,0:T(8,128)(2,1)}), bf16[256,2048]{1,0:T(8,128)(2,1)}) %reduce-scatter.17.cloned.1.call-update) | async-done | bytes 1048592 | tf_op jit(solution)/shard_map/reduce_scatter | solution.py:167
  1256.0 43.1 %all-reduce.2 = (f32[]{:T(128)}, f32[2048]{0:T(1024)}, f32[2048]{0:T(1024)}, f32[2048]{0:T(1024)S(1)}, f32[2048]{0:T(1024)S(1)}, /*index=5*/f32[2048]{0:T(1024)}...) all-reduce(f32[]{:T(128)} %get-tuple-element.543, ...), channel_id=1, replica_groups=mesh['fsdp'=8,'tp'=4] {'fsdp','tp'}, use_global_device_ids=true, to_apply=%region_15.16 | all-reduce | flops 24577 | bytes 196616 | tf_op jit(solution)/shard_map/psum | solution.py:234
  1301.7 3.3 add_add_fusion.2
  (324 shorter events, 99.4 us)
Async XLA Ops:
  7.2 5.1 copy-start.3
  7.2 33.3 %all-gather.14.cloned.1.call-start = ((), (), s32[]{:S(2)}) async-start(), calls=%async_computation.12 | async-start | bytes 2359296 | tf_op jit(solution)/shard_map/all_gather | solution.py:199
  8.0 115.5 %all-gather.10.cloned.1.call-start = ((), (), s32[]{:S(2)}) async-start(), calls=%async_computation.10 | async-start | bytes 5242880 | tf_op jit(solution)/shard_map/all_gather | solution.py:209
  11.7 6.3 copy-start.57
  13.7 137.9 %all-gather.16.cloned.1.call-start = ((), (), s32[]{:S(2)}) async-start(), calls=%async_computation.13 | async-start | bytes 2359296 | tf_op jit(solution)/shard_map/all_gather | solution.py:200
  14.5 166.8 %all-gather.12.cloned.1.call-start = ((), (), s32[]{:S(2)}) async-start(), calls=%async_computation.11 | async-start | bytes 2359296 | tf_op jit(solution)/shard_map/all_gather | solution.py:198
  15.0 210.4 %all-gather.18.cloned.1.call-start = ((), (), s32[]{:S(2)}) async-start(), calls=%async_computation.14 | async-start | bytes 2359296 | tf_op jit(solution)/shard_map/all_gather | solution.py:201
  15.6 293.1 %reduce-scatter.11.cloned.1.call-start = ((), (), s32[]{:S(2)}) async-start(), calls=%async_computation.15 | async-start | bytes 5242880 | tf_op jit(solution)/shard_map/reduce_scatter | solution.py:167
  18.1 133.5 %copy-start.64 = (f32[512]{0:T(512)S(1)}, f32[512]{0:T(512)}, u32[]{:S(2)}) copy-start(f32[512]{0:T(512)} %param.33) | copy-start | bytes 6148
  128.7 52.5 %copy-start.65 = (f32[512]{0:T(512)S(1)}, f32[512]{0:T(512)}, u32[]{:S(2)}) copy-start(f32[512]{0:T(512)} %param.30) | copy-start | bytes 6148
  222.0 9.8 copy-start.7
  225.4 6.4 copy-start.29
  231.8 77.0 %copy-start.4 = (bf16[256,2048]{1,0:T(8,128)(2,1)S(1)}, bf16[256,2048]{1,0:T(8,128)(2,1)}, u32[]{:S(2)}) copy-start(bf16[256,2048]{1,0:T(8,128)(2,1)} %param.26) | copy-start | bytes 3145732
  231.8 77.0 %copy-start.35 = (f32[2048]{0:T(1024)S(1)}, f32[2048]{0:T(1024)}, u32[]{:S(2)}) copy-start(f32[2048]{0:T(1024)} %param.35) | copy-start | bytes 24580
  231.8 189.8 %all-gather.22.cloned.1.call-start = ((), (), s32[]{:S(2)}) async-start(), calls=%async_computation.17 | async-start | bytes 9437184 | tf_op jit(solution)/shard_map/all_gather | solution.py:205
  232.6 78.5 %copy-start.40 = (f32[2048]{0:T(1024)S(1)}, f32[2048]{0:T(1024)}, u32[]{:S(2)}) copy-start(f32[2048]{0:T(1024)} %param.36) | copy-start | bytes 24580
  232.6 78.5 %copy-start.54 = (f32[2048]{0:T(1024)S(1)}, f32[2048]{0:T(1024)}, u32[]{:S(2)}) copy-start(f32[2048]{0:T(1024)} %param.37) | copy-start | bytes 24580
  232.6 230.3 %all-gather.20.cloned.1.call-start = ((), (), s32[]{:S(2)}) async-start(), calls=%async_computation.16 | async-start | bytes 5242880 | tf_op jit(solution)/shard_map/all_gather | solution.py:225
  233.0 15.2 %collective-permute-start = (bf16[256,2048]{1,0:T(8,128)(2,1)S(1)}, bf16[256,2048]{1,0:T(8,128)(2,1)}, u32[]{:S(2)}, u32[]{:S(2)}) collective-permute-start(bf16[256,2048]{1,0:T(8,128)(2,1)S(1)} %copy-done.24), channel_id=1, source_target_pairs={{0,4},{4,8},{8,12},{12,16},{16,20},{20,24},{24,28},{28,0},{1,5},{5... | collective-permute-start | bytes 3145736 | tf_op jit(solution)/shard_map/ppermute | solution.py:18
  248.2 64.6 %collective-permute-start.1 = (bf16[256,2048]{1,0:T(8,128)(2,1)}, bf16[256,2048]{1,0:T(8,128)(2,1)}, u32[]{:S(2)}, u32[]{:S(2)}) collective-permute-start(bf16[256,2048]{1,0:T(8,128)(2,1)} %collective-permute-done), channel_id=1, source_target_pairs={{0,4},{4,8},{8,12},{12,16},{16,20},{20,24},{24,28},{28,0},{1,5},{5... | collective-permute-start | bytes 3145736 | tf_op jit(solution)/shard_map/ppermute | solution.py:18
  312.8 253.8 %reduce-scatter.13.cloned.1.call-start = ((), (), s32[]{:S(2)}) async-start(), calls=%async_computation.18 | async-start | bytes 5242880 | tf_op jit(solution)/shard_map/reduce_scatter | solution.py:167
  312.8 27.0 %collective-permute-start.2 = (bf16[256,2048]{1,0:T(8,128)(2,1)}, bf16[256,2048]{1,0:T(8,128)(2,1)S(1)}, u32[]{:S(2)}, u32[]{:S(2)}) collective-permute-start(bf16[256,2048]{1,0:T(8,128)(2,1)} %collective-permute-done.1), channel_id=1, source_target_pairs={{0,4},{4,8},{8,12},{12,16},{16,20},{20,24},{24,28},{28,0},{1,5},{5... | collective-permute-start | bytes 3145736 | tf_op jit(solution)/shard_map/ppermute | solution.py:18
  340.8 32.6 %collective-permute-start.3 = (bf16[256,2048]{1,0:T(8,128)(2,1)S(1)}, bf16[256,2048]{1,0:T(8,128)(2,1)S(1)}, u32[]{:S(2)}, u32[]{:S(2)}) collective-permute-start(bf16[256,2048]{1,0:T(8,128)(2,1)S(1)} %collective-permute-done.2), channel_id=1, source_target_pairs={{0,4},{4,8},{8,12},{12,16},{16,20},{20,24},{24,28},{28,0},{1,5},{5... | collective-permute-start | bytes 3145736 | tf_op jit(solution)/shard_map/ppermute | solution.py:18
  374.4 15.4 %collective-permute-start.4 = (bf16[256,2048]{1,0:T(8,128)(2,1)S(1)}, bf16[256,2048]{1,0:T(8,128)(2,1)}, u32[]{:S(2)}, u32[]{:S(2)}) collective-permute-start(bf16[256,2048]{1,0:T(8,128)(2,1)S(1)} %collective-permute-done.3), channel_id=1, source_target_pairs={{0,4},{4,8},{8,12},{12,16},{16,20},{20,24},{24,28},{28,0},{1,5},{5... | collective-permute-start | bytes 3145736 | tf_op jit(solution)/shard_map/ppermute | solution.py:18
  389.8 15.4 %collective-permute-start.5 = (bf16[256,2048]{1,0:T(8,128)(2,1)}, bf16[256,2048]{1,0:T(8,128)(2,1)}, u32[]{:S(2)}, u32[]{:S(2)}) collective-permute-start(bf16[256,2048]{1,0:T(8,128)(2,1)} %collective-permute-done.4), channel_id=1, source_target_pairs={{0,4},{4,8},{8,12},{12,16},{16,20},{20,24},{24,28},{28,0},{1,5},{5... | collective-permute-start | bytes 3145736 | tf_op jit(solution)/shard_map/ppermute | solution.py:18
  395.1 12.4 copy-start.26
  397.5 11.1 copy-start.28
  405.2 15.3 %collective-permute-start.6 = (bf16[256,2048]{1,0:T(8,128)(2,1)}, bf16[256,2048]{1,0:T(8,128)(2,1)S(1)}, u32[]{:S(2)}, u32[]{:S(2)}) collective-permute-start(bf16[256,2048]{1,0:T(8,128)(2,1)} %collective-permute-done.5), channel_id=1, source_target_pairs={{0,4},{4,8},{8,12},{12,16},{16,20},{20,24},{24,28},{28,0},{1,5},{5... | collective-permute-start | bytes 3145736 | tf_op jit(solution)/shard_map/ppermute | solution.py:18
  412.0 51.0 %copy-start.63 = (f32[2048]{0:T(1024)S(1)}, f32[2048]{0:T(1024)}, u32[]{:S(2)}) copy-start(f32[2048]{0:T(1024)} %param.39) | copy-start | bytes 24580
  490.0 76.5 %copy-start.23 = (bf16[256,2048]{1,0:T(8,128)(2,1)S(1)}, bf16[256,2048]{1,0:T(8,128)(2,1)}, u32[]{:S(2)}) copy-start(bf16[256,2048]{1,0:T(8,128)(2,1)} %param.42) | copy-start | bytes 3145732
  490.0 76.5 %copy-start.56 = (f32[2048]{0:T(1024)S(1)}, f32[2048]{0:T(1024)}, u32[]{:S(2)}) copy-start(f32[2048]{0:T(1024)} %param.41) | copy-start | bytes 24580
  490.1 161.9 %all-gather.24.cloned.1.call-start = ((), (), s32[]{:S(2)}) async-start(), calls=%async_computation.19 | async-start | bytes 5242880 | tf_op jit(solution)/shard_map/all_gather | solution.py:241
  570.7 185.2 %reduce-scatter.15.cloned.1.call-start = ((), (), s32[]{:S(2)}) async-start(), calls=%async_computation.20 | async-start | bytes 5242880 | tf_op jit(solution)/shard_map/reduce_scatter | solution.py:167
  680.5 166.7 %all-gather.26.cloned.1.call-start = ((), (), s32[]{:S(2)}) async-start(), calls=%async_computation.21 | async-start | bytes 5242880 | tf_op jit(solution)/shard_map/all_gather | solution.py:260
  765.7 237.2 %reduce-scatter.29.cloned.1.call-start = ((), (), s32[]{:S(2)}) async-start(), calls=%async_computation.28 | async-start | bytes 9437184 | tf_op jit(solution)/shard_map/reduce_scatter | solution.py:252
  780.3 225.5 %reduce-scatter.27.cloned.1.call-start = ((), (), s32[]{:S(2)}) async-start(), calls=%async_computation.27 | async-start | bytes 9437184 | tf_op jit(solution)/shard_map/reduce_scatter | solution.py:249
  794.4 52.7 %copy-start.30 = (bf16[64,8,2,512]{3,1,2,0:T(8,128)(2,1)S(1)}, bf16[64,8,2,512]{3,1,2,0:T(8,128)(2,1)}, u32[]{:S(2)}) copy-start(bf16[64,8,2,512]{3,1,2,0:T(8,128)(2,1)} %copy-done.29) | copy-start | bytes 3145732
  794.4 245.3 %reduce-scatter.25.cloned.1.call-start = ((), (), s32[]{:S(2)}) async-start(), calls=%async_computation.26 | async-start | bytes 2359296 | tf_op jit(solution)/shard_map/reduce_scatter | solution.py:167
  853.1 8.2 copy-start.2
  853.1 8.2 copy-start.34
  853.1 8.2 copy-start.37
  853.1 8.2 copy-start.42
  853.2 8.1 copy-start.59
  853.2 8.1 copy-start.68
  853.2 230.9 %reduce-scatter.23.cloned.1.call-start = ((), (), s32[]{:S(2)}) async-start(), calls=%async_computation.25 | async-start | bytes 2359296 | tf_op jit(solution)/shard_map/reduce_scatter | solution.py:167
  866.8 9.9 copy-start.6
  870.4 6.2 copy-start
  895.3 12.6 copy-start.13
  917.8 9.3 copy-start.6
  921.4 5.7 copy-start
  948.0 13.3 %copy-start.13 = (bf16[2,512,8,64]{1,3,2,0:T(8,128)(2,1)S(1)}, bf16[2,512,8,64]{1,3,2,0:T(8,128)(2,1)}, u32[]{:S(2)}) copy-start(bf16[2,512,8,64]{1,3,2,0:T(8,128)(2,1)} %get-tuple-element.804) | copy-start | bytes 3145732 | tf_op jit(solution)/shard_map/while
  975.1 153.3 %reduce-scatter.19.cloned.1.call-start = ((), (), s32[]{:S(2)}) async-start(), calls=%async_computation.23 | async-start | bytes 2359296 | tf_op jit(solution)/shard_map/reduce_scatter | solution.py:167
  982.6 190.0 %reduce-scatter.21.cloned.1.call-start = ((), (), s32[]{:S(2)}) async-start(), calls=%async_computation.24 | async-start | bytes 2359296 | tf_op jit(solution)/shard_map/reduce_scatter | solution.py:167
  988.9 262.9 %reduce-scatter.17.cloned.1.call-start = ((), (), s32[]{:S(2)}) async-start(), calls=%async_computation.22 | async-start | bytes 5242880 | tf_op jit(solution)/shard_map/reduce_scatter | solution.py:167
  1008.7 243.1 %copy-start.5 = (bf16[256,2048]{1,0:T(8,128)(2,1)S(1)}, bf16[256,2048]{1,0:T(8,128)(2,1)}, u32[]{:S(2)}) copy-start(bf16[256,2048]{1,0:T(8,128)(2,1)} %param.26) | copy-start | bytes 3145732
  1008.7 243.1 %copy-start.39 = (f32[2048]{0:T(1024)S(1)}, f32[2048]{0:T(1024)}, u32[]{:S(2)}) copy-start(f32[2048]{0:T(1024)} %param.27) | copy-start | bytes 24580
  1008.7 243.1 %copy-start.44 = (f32[256]{0:T(256)S(1)}, f32[256]{0:T(256)}, u32[]{:S(2)}) copy-start(f32[256]{0:T(256)} %copy-done.43) | copy-start | bytes 3076
  1041.6 212.1 %copy-start.52 = (f32[256]{0:T(256)S(1)}, f32[256]{0:T(256)}, u32[]{:S(2)}) copy-start(f32[256]{0:T(256)} %copy-done.51) | copy-start | bytes 3076
  1041.6 212.1 %copy-start.50 = (f32[256]{0:T(256)S(1)}, f32[256]{0:T(256)}, u32[]{:S(2)}) copy-start(f32[256]{0:T(256)} %copy-done.49) | copy-start | bytes 3076
  1174.4 81.6 %copy-start.45 = (f32[2048]{0:T(1024)S(1)}, f32[2048]{0:T(1024)}, u32[]{:S(2)}) copy-start(f32[2048]{0:T(1024)} %get-tuple-element.460) | copy-start | bytes 24580
  1174.5 81.6 %copy-start.46 = (f32[2048]{0:T(1024)S(1)}, f32[2048]{0:T(1024)}, u32[]{:S(2)}) copy-start(f32[2048]{0:T(1024)} %get-tuple-element.454) | copy-start | bytes 24580
  1174.5 81.6 %copy-start.47 = (f32[2048]{0:T(1024)S(1)}, f32[2048]{0:T(1024)}, u32[]{:S(2)}) copy-start(f32[2048]{0:T(1024)} %get-tuple-element.528) | copy-start | bytes 24580
  1174.5 81.6 %copy-start.48 = (f32[2048]{0:T(1024)S(1)}, f32[2048]{0:T(1024)}, u32[]{:S(2)}) copy-start(f32[2048]{0:T(1024)} %get-tuple-element.544) | copy-start | bytes 24580
  1174.5 127.3 %copy-start.12 = (f32[256,2048]{1,0:T(8,128)S(1)}, f32[256,2048]{1,0:T(8,128)}, u32[]{:S(2)}) copy-start(f32[256,2048]{1,0:T(8,128)} %copy-done.11) | copy-start | bytes 6291460
  (41 other events, 98.9 us)
Sparse Core Ops, SparseCore 0:
  9.9 30.5 all-gather.13
  42.7 80.7 all-gather.9
  125.4 26.2 all-gather.15
  153.4 27.7 all-gather.11
  183.0 27.7 all-gather.17
  231.9 76.7 reduce-scatter.10
  310.6 69.7 all-gather.21
  382.6 80.2 all-gather.19
  490.2 76.3 reduce-scatter.12
  570.8 81.1 all-gather.23
  680.6 75.2 reduce-scatter.14
  765.8 81.2 all-gather.25
  850.6 69.9 reduce-scatter.28
  923.9 71.4 reduce-scatter.26
  998.6 41.1 reduce-scatter.24
  1042.9 41.1 reduce-scatter.22
  1087.2 41.1 reduce-scatter.18
  1131.5 41.1 reduce-scatter.20
  1174.9 76.7 reduce-scatter.16
